TPU v7x, 32 devices: a whole 2x2x4 slice. The times are simulated.
32 devices in a mesh: side: 4 (over y, core), batch: 8 (over z, x).
Axes of the slice: x: 2, y: 2, z: 4, core: 2. Of those that a mesh axis runs over, the one named last changes fastest.
Arguments:
- hidden_in: bfloat16 [4, 8, 1024, 512], P('side', 'batch'), may hold values from -6 to 6
- segments: int32 [4, 8, 1024], P('side', 'batch'), may hold values from -1 to 31, as said below
- query_cls: int32 [8, 32], P('batch'), may hold values from 0 to 930, as said below
- passage_cls: int32 [4, 8, 5], P('side', 'batch'), may hold values from 0 to 800, as said below
- pair_passage: int32 [256], P('batch'), may hold values from 0 to 119
- passage_cluster: int32 [120], replicated, may hold values from 0 to 31
- teacher: float32 [256, 120], P('batch'), may hold values from -6 to 6
- query_weight: bfloat16 [512, 512], replicated, may hold values from -0.25 to 0.25
- query_bias: float32 [512], replicated, may hold values from -3 to 3
- key_weight: bfloat16 [512, 512], replicated, may hold values from -0.25 to 0.25
- value_weight: bfloat16 [512, 512], replicated, may hold values from -0.25 to 0.25
- value_bias: float32 [512], replicated, may hold values from -1.75 to 1.75
- out_weight: bfloat16 [512, 512], replicated, may hold values from -1 to 1
- out_bias: float32 [512], replicated, may hold values from -1.75 to 1.75
- first_gain: float32 [512], replicated, may hold values from 0.5 to 1.5
- first_shift: float32 [512], replicated, may hold values from -1.75 to 1.75
- inner_weight: bfloat16 [512, 2048], replicated, may hold values from -0.25 to 0.25
- inner_bias: float32 [2048], replicated, may hold values from -3 to 3
- outer_weight: bfloat16 [2048, 512], replicated, may hold values from -0.125 to 0.125
- outer_bias: float32 [512], replicated, may hold values from -1.75 to 1.75
- second_gain: float32 [512], replicated, may hold values from 0.5 to 1.5
- second_shift: float32 [512], replicated, may hold values from -1.75 to 1.75
Outputs:
- loss: float32 [], replicated
- rows_out: bfloat16 [4, 8, 1024, 512], P('side', 'batch')
- input_grad: bfloat16 [4, 8, 1024, 512], P('side', 'batch')
- grad_query_weight: float32 [512, 512], replicated
- grad_query_bias: float32 [512], replicated
- grad_key_weight: float32 [512, 512], replicated
- grad_value_weight: float32 [512, 512], replicated
- grad_value_bias: float32 [512], replicated
- grad_out_weight: float32 [512, 512], replicated
- grad_out_bias: float32 [512], replicated
- grad_first_gain: float32 [512], replicated
- grad_first_shift: float32 [512], replicated
- grad_inner_weight: float32 [512, 2048], replicated
- grad_inner_bias: float32 [2048], replicated
- grad_outer_weight: float32 [2048, 512], replicated
- grad_outer_bias: float32 [512], replicated
- grad_second_gain: float32 [512], replicated
- grad_second_shift: float32 [512], replicated
Inputs may be any that keep to these rules, and one draw needn't show every extreme that they name: `segments`: in every row segment numbers start at 0 and never fall; the tokens after the last segment carry -1. A row of the first group holds 32 queries of 8 to 30 tokens, one of exactly 30; a row of another group holds 5 passages of 50 to 200 tokens, one of exactly 200. `query_cls`: the first token of each segment of the first group's row, in order. `passage_cls`: the first token of each passage of the row, in order; in the first group it holds the first 5 query starts, which nothing uses.
All inputs are finite; a program needn't handle non-finite values.
Results may differ from a plain program's by a relative error of at most 0.02.
Values may be sent and summed in bfloat16 or wider, within the bound.
No kernel may reach another device: no remote copies, remote signals or barrier semaphores. Data moves between devices by JAX's collectives and lax.ppermute only.
A program may use at most 192 MiB of HBM per device.

v0:
```python
from functools import partial
import jax
import jax.numpy as jnp
from jax import lax
from jax.sharding import PartitionSpec as P

HEADS = 8
HD = 64
EPSILON = 1e-05
NEG_FILL = -1e30


def norm_forward(summed, gain, shift):
    centre = jnp.mean(summed, axis=1, keepdims=True)
    deviation = summed - centre
    inverse = lax.rsqrt(jnp.mean(deviation * deviation, axis=1, keepdims=True) + EPSILON)
    normed = deviation * inverse
    return (normed * gain + shift, normed, inverse)


def norm_backward(upstream, normed, inverse, gain):
    scaled_up = upstream * gain
    inner_mean = jnp.mean(scaled_up, axis=1, keepdims=True)
    cross_mean = jnp.mean(scaled_up * normed, axis=1, keepdims=True)
    grad_in = inverse * (scaled_up - inner_mean - normed * cross_mean)
    return (grad_in, jnp.sum(upstream * normed, axis=0), jnp.sum(upstream, axis=0))


def contract_rows(left, right):
    return lax.dot_general(
        left, right, (((0,), (0,)), ((), ())), preferred_element_type=jnp.float32
    )


def times_transposed(left, right):
    return lax.dot_general(
        left, right, (((1,), (1,)), ((), ())), preferred_element_type=jnp.float32
    )


def block_scores(query_part, keys3, seg_part, seg_all, score_scale):
    raw = (
        jnp.einsum("qhd,khd->hqk", query_part, keys3, preferred_element_type=jnp.float32)
        * score_scale
    )
    same = seg_part[:, None] == seg_all[None, :]
    return jnp.where(same[None], raw, NEG_FILL)


def body(
    hidden_in,
    segments,
    query_cls,
    passage_cls,
    pair_passage,
    passage_cluster,
    teacher,
    query_weight,
    query_bias,
    key_weight,
    value_weight,
    value_bias,
    out_weight,
    out_bias,
    first_gain,
    first_shift,
    inner_weight,
    inner_bias,
    outer_weight,
    outer_bias,
    second_gain,
    second_shift,
):
    count_tok = hidden_in.shape[2]
    model_width = hidden_in.shape[3]
    tokens = hidden_in.reshape(count_tok, model_width)
    seg_ids = segments.reshape(count_tok)
    query_idx = query_cls.reshape(-1)
    passage_idx = passage_cls.reshape(-1)
    is_query = lax.axis_index("side") == 0
    score_scale = HD ** (-0.5)
    cls_scale = model_width ** (-0.5)
    block_rows = min(512, count_tok)
    queries = (
        jnp.dot(tokens, query_weight, preferred_element_type=jnp.float32) + query_bias
    ).astype(jnp.bfloat16)
    keys_low = jnp.dot(tokens, key_weight, preferred_element_type=jnp.float32).astype(jnp.bfloat16)
    values_low = (
        jnp.dot(tokens, value_weight, preferred_element_type=jnp.float32) + value_bias
    ).astype(jnp.bfloat16)
    queries3 = queries.reshape(count_tok, HEADS, HD)
    keys3 = keys_low.reshape(count_tok, HEADS, HD)
    values3 = values_low.reshape(count_tok, HEADS, HD)
    contexts = []
    log_parts = []
    for first_row in range(0, count_tok, block_rows):
        scores = block_scores(
            queries3[first_row : first_row + block_rows],
            keys3,
            seg_ids[first_row : first_row + block_rows],
            seg_ids,
            score_scale,
        )
        peak = jnp.max(scores, axis=2, keepdims=True)
        expo = jnp.exp(scores - peak)
        total = jnp.sum(expo, axis=2, keepdims=True)
        probs_low = (expo / total).astype(jnp.bfloat16)
        contexts.append(
            jnp.einsum("hqk,khd->qhd", probs_low, values3, preferred_element_type=jnp.float32)
        )
        log_parts.append(peak + jnp.log(total))
    context_low = (
        jnp.concatenate(contexts, axis=0).reshape(count_tok, model_width).astype(jnp.bfloat16)
    )
    log_totals = jnp.concatenate(log_parts, axis=1)
    attended = tokens.astype(jnp.float32) + (
        jnp.dot(context_low, out_weight, preferred_element_type=jnp.float32) + out_bias
    )
    first, first_hat, first_inv = norm_forward(attended, first_gain, first_shift)
    first_low = first.astype(jnp.bfloat16)
    pre = jnp.dot(first_low, inner_weight, preferred_element_type=jnp.float32) + inner_bias
    gelu_exact = partial(jax.nn.gelu, approximate=False)
    activated, gelu_pull = jax.vjp(gelu_exact, pre)
    active_low = activated.astype(jnp.bfloat16)
    second = first + (
        jnp.dot(active_low, outer_weight, preferred_element_type=jnp.float32) + outer_bias
    )
    final, second_hat, second_inv = norm_forward(second, second_gain, second_shift)
    final_low = final.astype(jnp.bfloat16)
    query_vectors = final_low[query_idx]
    passage_vectors = final_low[passage_idx]
    gathered = lax.all_gather(passage_vectors, ("side", "batch"), axis=0, tiled=True)
    pass_count = teacher.shape[1]
    front = gathered.shape[0] - pass_count
    passages_all = gathered[front:]
    scores_cls = times_transposed(query_vectors, passages_all) * cls_scale
    columns = jnp.arange(pass_count, dtype=jnp.int32)
    is_pair = pair_passage[:, None] == columns[None, :]
    query_cluster = jnp.sum(jnp.where(is_pair, passage_cluster[None, :], 0), axis=1)
    counted = (
        (passage_cluster[None, :] == query_cluster[:, None]) & jnp.logical_not(is_pair) & is_query
    )
    pair_score = jnp.sum(jnp.where(is_pair, scores_cls, 0.0), axis=1, keepdims=True)
    resid = jnp.where(counted, pair_score - scores_cls - teacher, 0.0)
    loss_sq = jnp.sum(resid * resid)
    loss_count = jnp.sum(counted.astype(jnp.float32))
    grad_score = jnp.where(is_pair, jnp.sum(resid, axis=1, keepdims=True), 0.0) - resid
    grad_score_low = (grad_score * cls_scale).astype(jnp.bfloat16)
    grad_queries = jnp.dot(grad_score_low, passages_all, preferred_element_type=jnp.float32)
    padded = jnp.concatenate(
        [jnp.zeros((front, grad_score_low.shape[0]), jnp.bfloat16), grad_score_low.T], axis=0
    )
    grad_passages = lax.psum_scatter(
        jnp.dot(
            lax.slice_in_dim(
                padded, 0, passage_vectors.shape[0] * lax.axis_size(("side", "batch")), axis=0
            ),
            query_vectors,
            preferred_element_type=jnp.float32,
        ),
        ("side", "batch"),
        scatter_dimension=0,
        tiled=True,
    )
    zero_rows = jnp.zeros((count_tok, model_width), jnp.float32)
    grad_final = jnp.where(
        is_query,
        zero_rows.at[query_idx].add(grad_queries),
        zero_rows.at[passage_idx].add(grad_passages),
    )
    grad_second, grad_second_gain, grad_second_shift = norm_backward(
        grad_final, second_hat, second_inv, second_gain
    )
    grad_outer_bias = jnp.sum(grad_second, axis=0)
    second_low = grad_second.astype(jnp.bfloat16)
    grad_outer_weight = contract_rows(active_low, second_low)
    grad_active = times_transposed(second_low, outer_weight)
    grad_pre = gelu_pull(grad_active)[0]
    grad_inner_bias = jnp.sum(grad_pre, axis=0)
    pre_low = grad_pre.astype(jnp.bfloat16)
    grad_inner_weight = contract_rows(first_low, pre_low)
    grad_first = times_transposed(pre_low, inner_weight) + grad_second
    ffn_parts = (
        grad_inner_weight,
        grad_inner_bias,
        grad_outer_weight,
        grad_outer_bias,
        grad_second_gain,
        grad_second_shift,
    )
    grad_attended, grad_first_gain, grad_first_shift = norm_backward(
        grad_first, first_hat, first_inv, first_gain
    )
    grad_out_bias = jnp.sum(grad_attended, axis=0)
    attended_low = grad_attended.astype(jnp.bfloat16)
    grad_out_weight = contract_rows(context_low, attended_low)
    grad_context = times_transposed(attended_low, out_weight).astype(jnp.bfloat16)
    grad_context3 = grad_context.reshape(count_tok, HEADS, HD)
    grad_query_parts = []
    grad_keys = jnp.zeros((count_tok, HEADS, HD), jnp.float32)
    grad_values = jnp.zeros((count_tok, HEADS, HD), jnp.float32)
    for first_row in range(0, count_tok, block_rows):
        query_part = queries3[first_row : first_row + block_rows]
        scores = block_scores(
            query_part, keys3, seg_ids[first_row : first_row + block_rows], seg_ids, score_scale
        )
        probs = jnp.exp(scores - log_totals[:, first_row : first_row + block_rows])
        upstream = grad_context3[first_row : first_row + block_rows]
        grad_probs = jnp.einsum(
            "qhd,khd->hqk", upstream, values3, preferred_element_type=jnp.float32
        )
        row_dot = jnp.sum(probs * grad_probs, axis=2, keepdims=True)
        grad_scores = (probs * (grad_probs - row_dot)).astype(jnp.bfloat16)
        grad_query_parts.append(
            jnp.einsum("hqk,khd->qhd", grad_scores, keys3, preferred_element_type=jnp.float32)
            * score_scale
        )
        grad_keys = (
            grad_keys
            + jnp.einsum(
                "hqk,qhd->khd", grad_scores, query_part, preferred_element_type=jnp.float32
            )
            * score_scale
        )
        grad_values = grad_values + jnp.einsum(
            "hqk,qhd->khd", probs.astype(jnp.bfloat16), upstream, preferred_element_type=jnp.float32
        )
    grad_query = jnp.concatenate(grad_query_parts, axis=0).reshape(count_tok, model_width)
    grad_keys = grad_keys.reshape(count_tok, model_width)
    grad_values = grad_values.reshape(count_tok, model_width)
    grad_query_bias = jnp.sum(grad_query, axis=0)
    grad_value_bias = jnp.sum(grad_values, axis=0)
    query_low = grad_query.astype(jnp.bfloat16)
    key_low = grad_keys.astype(jnp.bfloat16)
    value_low = grad_values.astype(jnp.bfloat16)
    grad_query_weight = contract_rows(hidden_in.reshape(count_tok, model_width), query_low)
    grad_key_weight = contract_rows(tokens, key_low)
    grad_value_weight = contract_rows(tokens, value_low)
    input_grad = (
        grad_attended
        + times_transposed(query_low, query_weight)
        + times_transposed(key_low, key_weight)
        + times_transposed(value_low, value_weight)
    ).astype(jnp.bfloat16)
    attention_parts = (
        grad_query_weight,
        grad_query_bias,
        grad_key_weight,
        grad_value_weight,
        grad_value_bias,
        grad_out_weight,
        grad_out_bias,
        grad_first_gain,
        grad_first_shift,
    )
    summed_all = lax.psum(
        (
            grad_query_weight,
            grad_query_bias,
            grad_key_weight,
            grad_value_weight,
            grad_value_bias,
            grad_out_weight,
            grad_out_bias,
            grad_first_gain,
            grad_first_shift,
            grad_inner_weight,
            grad_inner_bias,
            grad_outer_weight,
            grad_outer_bias,
            grad_second_gain,
            grad_second_shift,
            loss_sq,
            loss_count,
        ),
        ("side", "batch"),
    )
    attention_parts = summed_all[:9]
    ffn_parts = summed_all[9:15]
    loss_sq = summed_all[15]
    loss_count = summed_all[16]
    loss = loss_sq / jnp.maximum(loss_count, 1.0)
    rows_out = final_low.reshape(1, 1, count_tok, model_width)
    input_grad = input_grad.reshape(1, 1, count_tok, model_width)
    return (
        loss,
        rows_out,
        input_grad,
        attention_parts[0],
        attention_parts[1],
        attention_parts[2],
        attention_parts[3],
        attention_parts[4],
        attention_parts[5],
        attention_parts[6],
        attention_parts[7],
        attention_parts[8],
        ffn_parts[0],
        ffn_parts[1],
        ffn_parts[2],
        ffn_parts[3],
        ffn_parts[4],
        ffn_parts[5],
    )


def solution(mesh):
    in_specs = (
        P("side", "batch", None, None),
        P("side", "batch", None),
        P("batch", None),
        P("side", "batch", None),
        P("batch"),
        P(),
        P("batch", None),
        P(),
        P(),
        P(),
        P(),
        P(),
        P(),
        P(),
        P(),
        P(),
        P(),
        P(),
        P(),
        P(),
        P(),
        P(),
    )
    out_specs = (
        P(),
        P("side", "batch", None, None),
        P("side", "batch", None, None),
        P(),
        P(),
        P(),
        P(),
        P(),
        P(),
        P(),
        P(),
        P(),
        P(),
        P(),
        P(),
        P(),
        P(),
        P(),
    )
    return jax.shard_map(body, mesh=mesh, in_specs=in_specs, out_specs=out_specs, check_vma=False)
```

profile of v0, /device:TPU:0, one launch (start us, length us, event | category | flops | bytes accessed | tf_op | source)
XLA Modules:
  0.0 664.5 jit_solution(5748049418920462220)
XLA Ops:
  7.3 0.8 fusion.61
  9.5 2.3 copy.70
  11.8 2.2 add_convert_fusion.2
  14.2 0.8 convolution_convert_fusion.1
  15.0 0.8 add_convert_fusion.3
  16.4 3.2 fusion.79
  19.7 3.5 fusion.1
  23.2 2.2 copy-done.1
  25.4 3.8 fusion.35
  29.2 3.2 fusion.80
  32.4 3.5 fusion
  36.0 2.2 copy-done.2
  38.2 4.0 fusion.34
  42.4 1.0 copy-done.21
  43.3 0.8 fusion.81
  44.5 23.8 %multiply_convert_fusion.2 = (bf16[1024,2048]{1,0:T(8,128)(2,1)S(1)}, f32[1024,2048]{1,0:T(8,128)}, f32[1024,2048]{1,0:T(8,128)}) fusion(f32[2048]{0:T(1024)S(1)} %copy-done.59, bf16[512,2048]{1,0:T(8,128)(2,1)S(1)} %copy-done, f32[1024,512]{0,1:T(8,128)S(1)} %get-tuple-element.126, f32[512]{0:T(512)S(1)} %copy-done.63, f32[512]{0:T(512)S(1)} %copy-done.53, ...), kind=kOutput, calls=%fused_computation.27 | convolution fusion | flops 2288517120 | bytes 25186304 | tf_op jit(solution)/shard_map/dot_general | solution.py:121
  68.4 2.7 fusion.82
  71.5 1.0 copy-done.4
  72.8 1.3 copy.72
  74.2 1.9 gather_fusion.1
  76.1 2.0 gather_fusion
  78.1 71.2 %all-gather.1 = bf16[32,5,512]{2,1,0:T(8,128)(2,1)S(1)} all-gather(bf16[1,5,512]{2,1,0:T(8,128)(2,1)S(1)} %bitcast.146), channel_id=2, replica_groups=mesh['side'=4,'batch'=8] {'side','batch'}, dimensions={0}, use_global_device_ids=true | all-gather | bytes 168960 | tf_op jit(solution)/shard_map/all_gather | solution.py:132
  151.0 1.0 fusion.56
  152.9 2.2 scatter_custom_fusion
  155.1 2.9 copy.74
  158.1 115.9 %all-reduce.7.cloned.1.call-done = f32[160,512]{1,0:T(8,128)} async-done(((f32[160,512]{1,0:T(8,128)}), f32[160,512]{1,0:T(8,128)}) %all-reduce.7.cloned.1.call-update) | async-done | bytes 327696
  274.0 2.3 scatter_custom_fusion.1
  276.2 3.0 copy.75
  279.3 3.9 multiply_reduce_fusion.2
  283.2 1.3 fusion.71
  284.5 0.8 copy-done.65
  285.4 4.5 fusion.52
  289.9 9.7 %fusion.83 = (f32[2048]{0:T(1024)}, bf16[1024,2048]{1,0:T(8,128)(2,1)S(1)}) fusion(f32[1024,2048]{1,0:T(8,128)} %get-tuple-element.108, bf16[2048,512]{1,0:T(8,128)(2,1)S(1)} %copy-done.58, f32[1024,512]{0,1:T(8,128)S(1)} %get-tuple-element.102, f32[1024,2048]{1,0:T(8,128)} %get-tuple-element.127, f32[2048]{0:T(1024)S(1)} %copy-done.59), kind=kOutput, calls=%fused_computation.157 | convolution fusion | flops 2181560320 | bytes 25182208 | tf_op jit(solution)/shard_map/dot_general | solution.py:36
  299.6 3.7 multiply_reduce_fusion.3
  303.3 4.5 fusion.18
  307.8 1.4 fusion.72
  309.2 1.7 fusion.49
  311.7 0.9 fusion.76
  313.1 9.9 %multiply_reduce_fusion.1 = (f32[8,512]{1,0:T(8,128)}, f32[8,512,1024]{2,1,0:T(8,128)}) fusion(f32[8,512,1024]{2,1,0:T(8,128)S(1)} %bitcast.120, f32[8,512]{1,0:T(8,128)S(1)} %log_add_fusion.1, bf16[512,8,64]{0,2,1:T(8,128)(2,1)S(1)} %bitcast.131, bf16[1024,8,64]{0,2,1:T(8,128)(2,1)} %bitcast.137), kind=kOutput, calls=%fused_computation.8 | convolution fusion | flops 549449728 | bytes 35160064 | tf_op jit(solution)/shard_map/qhd,khd->hqk/dot_general | solution.py:209
  323.0 15.9 %multiply_convert_fusion.1 = bf16[8,512,1024]{2,1,0:T(8,128)(2,1)} fusion(f32[8,512,1024]{2,1,0:T(8,128)} %get-tuple-element.133, f32[8,512,1024]{2,1,0:T(8,128)} %copy-done.2, f32[8,512]{1,0:T(8,128)} %get-tuple-element.132, f32[8,512]{1,0:T(8,128)S(1)} %log_add_fusion.1), kind=kLoop, calls=%fused_computation.7 | loop fusion | flops 16777216 | bytes 41975808 | tf_op jit(solution)/shard_map/convert_element_type | solution.py:213
  338.9 8.2 %fusion.74 = (bf16[512,8,64]{0,2,1:T(8,128)(2,1)}, f32[8,64]{1,0:T(8,128)}) fusion(bf16[1024,8,64]{0,2,1:T(8,128)(2,1)S(1)} %bitcast.124, bf16[8,512,1024]{2,1,0:T(8,128)(2,1)} %multiply_convert_fusion.1), kind=kOutput, calls=%fused_computation.148 | convolution fusion | flops 537656832 | bytes 9963520 | tf_op jit(solution)/shard_map/hqk,khd->qhd/dot_general | solution.py:215
  347.2 6.3 fusion.84
  353.6 4.0 fusion.5
  357.6 9.9 %multiply_reduce_fusion = (f32[8,512]{1,0:T(8,128)}, f32[8,512,1024]{2,1,0:T(8,128)}) fusion(f32[8,512,1024]{2,1,0:T(8,128)S(1)} %bitcast.118, f32[8,512]{1,0:T(8,128)} %log_add_fusion, bf16[512,8,64]{0,2,1:T(8,128)(2,1)} %bitcast.133, bf16[1024,8,64]{0,2,1:T(8,128)(2,1)} %bitcast.138), kind=kOutput, calls=%fused_computation.5 | convolution fusion | flops 549449728 | bytes 35160064 | tf_op jit(solution)/shard_map/qhd,khd->hqk/dot_general | solution.py:209
  367.5 8.8 %bitcast_reduce_fusion = (f32[8,64]{1,0:T(8,128)}, bf16[8,64,1024]{2,1,0:T(8,128)(2,1)S(1)}) fusion(f32[8,64,1024]{2,1,0:T(8,128)} %fusion.5, bf16[512,8,64]{0,2,1:T(8,128)(2,1)S(1)} %bitcast.132, f32[8,512,1024]{2,1,0:T(8,128)} %copy-done.2, f32[8,512]{1,0:T(8,128)S(1)} %log_add_fusion.1), kind=kOutput, calls=%fused_computation.43 | convolution fusion | flops 546831872 | bytes 20465664 | tf_op jit(solution)/shard_map/hqk,qhd->khd/dot_general | solution.py:225
  376.3 1.8 convolution_bitcast_fusion
  378.1 10.5 %multiply_convert_fusion = bf16[8,512,1024]{2,1,0:T(8,128)(2,1)} fusion(f32[8,512,1024]{2,1,0:T(8,128)} %get-tuple-element.135, f32[8,512,1024]{2,1,0:T(8,128)S(1)} %bitcast.118, f32[8,512]{1,0:T(8,128)S(1)} %copy-done.38, f32[8,512]{1,0:T(8,128)S(1)} %copy-done.37), kind=kLoop, calls=%fused_computation.4 | loop fusion | flops 16777216 | bytes 41975808 | tf_op jit(solution)/shard_map/convert_element_type | solution.py:213
  388.6 6.6 fusion.75
  395.3 3.4 multiply_convert_fusion.3
  398.6 1.7 convolution_bitcast_fusion.1
  400.3 1.7 convolution_bitcast_fusion.2
  402.8 2.9 fusion.134
  405.7 2.3 copy.80
  408.2 43.7 %all-reduce.2 = (f32[]{:T(128)}, f32[]{:T(128)}, f32[512]{0:T(512)}, f32[512]{0:T(512)}, f32[512]{0:T(512)}, /*index=5*/f32[512]{0:T(512)}, f32[512]{0:T(512)}, ...) all-reduce(f32[]{:T(128)} %get-tuple-element.81, ...), channel_id=1, replica_groups=mesh['side'=4,'batch'=8] {'side','batch'}, use_global_device_ids=true, to_apply=%region_11.12 | all-reduce | flops 6146 | bytes 49168 | tf_op jit(solution)/shard_map/psum | solution.py:256
  451.9 1.4 pad_maximum_fusion.1
  453.3 1.9 fusion.86
  456.8 1.3 copy.81
  459.4 181.1 %all-reduce.9.cloned.1.call-done = (f32[512,512]{0,1:T(8,128)}, f32[512,512]{0,1:T(8,128)}, f32[512,512]{0,1:T(8,128)}, f32[512,512]{1,0:T(8,128)}, f32[512,2048]{1,0:T(8,128)}, /*index=5*/f32[2048,512]{1,0:T(8,128)}) async-done(((f32[512,512]{0,1:T(8,128)}, f32[512,512]{0,1:T(8,128)}, f32[512,512]{0,1:T(8,128)}, f32[512,512]{1,0:T(8,128)}, f32[512,2048]{1,0:T(8,128)}, /*index=5*/f32[2048,512]{1,0:T(8,128)}), ...) | async-done | bytes 12582928 | tf_op jit(solution)/shard_map/psum | solution.py:256
  640.5 2.6 copy.82
  643.1 2.5 copy.83
  645.6 2.5 copy.84
  648.2 1.0 copy.97
  649.2 4.8 copy.98
  654.0 2.0 copy.99
  (181 shorter events, 9.7 us)
Async XLA Ops:
  7.2 37.3 %copy-start = (bf16[512,2048]{1,0:T(8,128)(2,1)S(1)}, bf16[512,2048]{1,0:T(8,128)(2,1)}, u32[]{:S(2)}) copy-start(bf16[512,2048]{1,0:T(8,128)(2,1)} %param.38) | copy-start | bytes 6291460
  7.2 6.9 %copy-start.25 = (bf16[1,1,1024,512]{3,2,1,0:T(8,128)(2,1)S(1)}, bf16[1,1,1024,512]{3,2,1,0:T(8,128)(2,1)}, u32[]{:S(2)}) copy-start(bf16[1,1,1024,512]{3,2,1,0:T(8,128)(2,1)} %param.22) | copy-start | bytes 3145732
  7.2 266.8 %all-reduce.7.cloned.1.call-start = ((), (), s32[]{:S(2)}) async-start(), calls=%async_computation | async-start | bytes 655360
  11.8 3.1 copy-start.34
  11.8 3.1 copy-start.60
  14.2 5.5 copy-start.12
  14.2 15.0 %copy-start.14 = (bf16[512,512]{0,1:T(8,128)(2,1)}, bf16[512,512]{0,1:T(8,128)(2,1)S(1)}, u32[]{:S(2)}) copy-start(bf16[512,512]{0,1:T(8,128)(2,1)S(1)} %get-tuple-element.115) | copy-start | bytes 1572868
  15.0 14.3 %copy-start.8 = (bf16[1024,512]{0,1:T(8,128)(2,1)}, bf16[1024,512]{0,1:T(8,128)(2,1)S(1)}, u32[]{:S(2)}) copy-start(bf16[1024,512]{0,1:T(8,128)(2,1)S(1)} %convolution_convert_fusion.1) | copy-start | bytes 3145732
  15.7 20.2 %copy-start.17 = (bf16[1024,512]{0,1:T(8,128)(2,1)}, bf16[1024,512]{0,1:T(8,128)(2,1)S(1)}, u32[]{:S(2)}) copy-start(bf16[1024,512]{0,1:T(8,128)(2,1)S(1)} %add_convert_fusion.3) | copy-start | bytes 3145732
  19.7 5.7 copy-start.1
  32.4 5.7 copy-start.2
  38.2 5.2 copy-start.29
  38.2 5.2 copy-start.30
  38.2 5.2 copy-start.61
  44.1 24.2 %copy-start.10 = (f32[1024,512]{0,1:T(8,128)}, f32[1024,512]{0,1:T(8,128)S(1)}, u32[]{:S(2)}) copy-start(f32[1024,512]{0,1:T(8,128)S(1)} %get-tuple-element.126) | copy-start | bytes 6291460
  44.5 23.9 %copy-start.57 = (bf16[2048,512]{1,0:T(8,128)(2,1)S(1)}, bf16[2048,512]{1,0:T(8,128)(2,1)}, u32[]{:S(2)}) copy-start(bf16[2048,512]{1,0:T(8,128)(2,1)} %param.40) | copy-start | bytes 6291460
  44.5 23.9 %copy-start.62 = (f32[512]{0:T(512)S(1)}, f32[512]{0:T(512)}, u32[]{:S(2)}) copy-start(f32[512]{0:T(512)} %param.41) | copy-start | bytes 6148
  68.4 2.7 copy-start.64
  68.4 4.1 copy-start.39
  68.4 4.1 copy-start.45
  71.1 78.2 %copy-start.52 = (s32[32]{0:T(128)S(1)}, s32[32]{0:T(128)}, u32[]{:S(2)}) copy-start(s32[32]{0:T(128)} %param.26) | copy-start | bytes 388
  71.2 78.2 %copy-start.56 = (s32[120]{0:T(128)S(1)}, s32[120]{0:T(128)}, u32[]{:S(2)}) copy-start(s32[120]{0:T(128)} %param.27) | copy-start | bytes 1444
  71.2 79.1 %copy-start.44 = (f32[32,120]{1,0:T(8,128)S(1)}, f32[32,120]{1,0:T(8,128)}, u32[]{:S(2)}) copy-start(f32[32,120]{1,0:T(8,128)} %param.28) | copy-start | bytes 46084
  152.1 488.4 %all-reduce.9.cloned.1.call-start = ((), (), s32[]{:S(2)}) async-start(), calls=%async_computation.1 | async-start | bytes 25165824 | tf_op jit(solution)/shard_map/psum | solution.py:256
  279.3 3.9 copy-start.5
  285.3 4.5 copy-start.58
  289.9 9.7 %copy-start.11 = (f32[1024,512]{0,1:T(8,128)S(1)}, f32[1024,512]{0,1:T(8,128)}, u32[]{:S(2)}) copy-start(f32[1024,512]{0,1:T(8,128)} %copy-done.10) | copy-start | bytes 6291460
  303.3 9.3 %slice-start.4 = ((s8[16777216]{0:T(1024)(128)(4,1)}), s8[4194304]{0:T(1024)(128)(4,1)S(1)}, s32[]{:S(2)}) async-start(s8[16777216]{0:T(1024)(128)(4,1)} %bitcast.119), calls=%async_computation.6 | async-start | bytes 8388608
  303.3 9.3 %slice-start.5 = ((s8[16777216]{0:T(1024)(128)(4,1)}), s8[4194304]{0:T(1024)(128)(4,1)S(1)}, s32[]{:S(2)}) async-start(s8[16777216]{0:T(1024)(128)(4,1)} %bitcast.119), calls=%async_computation.7 | async-start | bytes 8388608
  307.8 3.1 copy-start.31
  307.8 4.7 slice-start.6
  309.2 3.3 copy-start.6
  309.2 3.9 slice-start.7
  322.9 16.0 %copy-start.9 = (bf16[1024,512]{0,1:T(8,128)(2,1)S(1)}, bf16[1024,512]{0,1:T(8,128)(2,1)}, u32[]{:S(2)}) copy-start(bf16[1024,512]{0,1:T(8,128)(2,1)} %copy-done.8) | copy-start | bytes 3145732
  322.9 30.6 %slice-start = ((s8[16777216]{0:T(1024)(128)(4,1)}), s8[4194304]{0:T(1024)(128)(4,1)S(1)}, s32[]{:S(2)}) async-start(s8[16777216]{0:T(1024)(128)(4,1)} %bitcast.117), calls=%async_computation.2 | async-start | bytes 8388608
  322.9 30.6 %slice-start.1 = ((s8[16777216]{0:T(1024)(128)(4,1)}), s8[4194304]{0:T(1024)(128)(4,1)S(1)}, s32[]{:S(2)}) async-start(s8[16777216]{0:T(1024)(128)(4,1)} %bitcast.117), calls=%async_computation.3 | async-start | bytes 8388608
  323.0 30.6 %slice-start.2 = ((s8[16777216]{0:T(1024)(128)(4,1)}), s8[4194304]{0:T(1024)(128)(4,1)S(1)}, s32[]{:S(2)}) async-start(s8[16777216]{0:T(1024)(128)(4,1)} %bitcast.117), calls=%async_computation.4 | async-start | bytes 8388608
  338.9 8.2 %copy-start.15 = (bf16[512,512]{0,1:T(8,128)(2,1)S(1)}, bf16[512,512]{0,1:T(8,128)(2,1)}, u32[]{:S(2)}) copy-start(bf16[512,512]{0,1:T(8,128)(2,1)} %copy-done.14) | copy-start | bytes 1572868
  338.9 14.6 %slice-start.3 = ((s8[16777216]{0:T(1024)(128)(4,1)}), s8[4194304]{0:T(1024)(128)(4,1)S(1)}, s32[]{:S(2)}) async-start(s8[16777216]{0:T(1024)(128)(4,1)} %bitcast.117), calls=%async_computation.5 | async-start | bytes 8388608
  347.2 6.4 copy-start.16
  347.2 6.4 copy-start.36
  367.5 8.8 %copy-start.26 = (bf16[1,1,1024,512]{3,2,1,0:T(8,128)(2,1)S(1)}, bf16[1,1,1024,512]{3,2,1,0:T(8,128)(2,1)}, u32[]{:S(2)}) copy-start(bf16[1,1,1024,512]{3,2,1,0:T(8,128)(2,1)} %param.22) | copy-start | bytes 3145732
  367.5 10.6 %copy-start.37 = (f32[8,512]{1,0:T(8,128)S(1)}, f32[8,512]{1,0:T(8,128)}, u32[]{:S(2)}) copy-start(f32[8,512]{1,0:T(8,128)} %log_add_fusion) | copy-start | bytes 49156
  367.5 10.6 %copy-start.38 = (f32[8,512]{1,0:T(8,128)S(1)}, f32[8,512]{1,0:T(8,128)}, u32[]{:S(2)}) copy-start(f32[8,512]{1,0:T(8,128)} %get-tuple-element.134) | copy-start | bytes 49156
  388.6 6.6 copy-start.3
  388.6 6.6 copy-start.13
  395.2 5.1 copy-start.24
  395.2 3.4 copy-start.27
  395.2 5.1 copy-start.23
  402.7 5.3 copy-start.43
  402.7 5.4 copy-start.41
  402.7 5.5 copy-start.47
  402.7 5.5 copy-start.48
  402.7 5.5 copy-start.49
  402.7 5.4 copy-start.50
  402.8 5.4 copy-start.51
  402.8 5.4 copy-start.54
  402.8 5.4 copy-start.55
  451.9 3.3 copy-start.33
  453.3 2.7 copy-start.7
  453.3 2.7 copy-start.19
  453.3 2.7 copy-start.35
  640.5 7.7 %copy-start.28 = (f32[512,512]{1,0:T(8,128)S(1)}, f32[512,512]{1,0:T(8,128)}, u32[]{:S(2)}) copy-start(f32[512,512]{1,0:T(8,128)} %get-tuple-element.156) | copy-start | bytes 3145732
  649.1 4.9 copy-start.20
  (12 other events, 20.0 us)
Sparse Core Ops, SparseCore 0:
  152.2 121.7 all-reduce.6
  402.2 238.2 all-reduce.8
where the time goes:
time: 674 us; the launch traced here: 664 us
  waiting for transfers between devices  297 us (44%)
  matrix products  138 us (20%)
  blocking collectives  115 us (17%)
  other arithmetic  53.7 us (8%)
  local copies, waits for them, and re-layouts  43.2 us (6%)
  between operations  17.9 us (3%)
    psum x1, waiting for transfers between devices, body(): lax.psum((grad_query_weight, grad_query_bias, grad_key_weight, grad_value...  181 us
    unnamed x3, waiting for transfers between devices  116 us
    all_gather x1, blocking collectives, body(): lax.all_gather(passage_vectors, ('side', 'batch'), axis=0, tiled=True)  71.2 us
    psum x1, blocking collectives, body(): lax.psum((grad_query_weight, grad_query_bias, grad_key_weight, grad_value...  43.7 us
    unnamed x157, local copies, waits for them, and re-layouts  30.1 us
    convert_element_type x2, other arithmetic, body(): grad_scores = (probs * (grad_probs - row_dot)).astype(jnp.bfloat16)  26.4 us
    dot_general x1, matrix products, body(): jnp.dot(first_low, inner_weight, preferred_element_type=jnp.float32)  23.8 us
    dot_general x2, matrix products, body(): jnp.einsum('qhd,khd->hqk', upstream, values3, preferred_element_type=jnp....  19.8 us
  transfers between devices with their start and end apart: 2, of which 2 were waited for; matrix products, arithmetic and copies ran while one was open for 3% of the time, Pallas kernels for 0%

commit v1 on v0

--- a/solution.py
+++ b/solution.py
@@ -253,7 +253,7 @@
         grad_first_gain,
         grad_first_shift,
     )
-    summed_all = lax.psum(
+    inner = lax.psum(
         (
             grad_query_weight,
             grad_query_bias,
@@ -273,8 +273,9 @@
             loss_sq,
             loss_count,
         ),
-        ("side", "batch"),
-    )
+        "batch",
+    )
+    summed_all = lax.psum(inner, "side")
     attention_parts = summed_all[:9]
     ffn_parts = summed_all[9:15]
     loss_sq = summed_all[15]

time: 674 us -> 1060 us (1.57)
  waiting for transfers between devices: 297 us -> 683 us
    psum x1, waiting for transfers between devices: 181 us -> 404 us  [body(): lax.psum((grad_query_weight, grad_query_bias, grad_key_weight, grad_value...]
    psum x0 -> x1, waiting for transfers between devices: none -> 163 us  [body(): summed_all = lax.psum(inner, 'side')]
    psum x0 -> x1, blocking collectives: none -> 13 us  [body(): summed_all = lax.psum(inner, 'side')]
    unnamed x157 -> x163, local copies, waits for them, and re-layouts: 30.1 us -> 29.9 us
    unnamed x3 -> x4, waiting for transfers between devices: 116 us -> 116 us
  transfers between devices with their start and end apart: 2 -> 3, of which waited for: 2 -> 3; matrix products, arithmetic and copies ran while one was open for 3% -> 2% of each run, Pallas kernels for 0% -> 0%
where the time goes in v1:
time: 1060 us; the launch traced here: 1050 us
  waiting for transfers between devices  683 us (64%)
  matrix products  138 us (13%)
  blocking collectives  119 us (11%)
  other arithmetic  52.1 us (5%)
  local copies, waits for them, and re-layouts  42.9 us (4%)
  between operations  17.6 us (2%)
    psum x1, waiting for transfers between devices, body(): lax.psum((grad_query_weight, grad_query_bias, grad_key_weight, grad_value...  404 us
    psum x1, waiting for transfers between devices, body(): summed_all = lax.psum(inner, 'side')  163 us
    unnamed x4, waiting for transfers between devices  116 us
    all_gather x1, blocking collectives, body(): lax.all_gather(passage_vectors, ('side', 'batch'), axis=0, tiled=True)  71.2 us
    psum x1, blocking collectives, body(): lax.psum((grad_query_weight, grad_query_bias, grad_key_weight, grad_value...  34.5 us
    unnamed x163, local copies, waits for them, and re-layouts  29.9 us
    convert_element_type x2, other arithmetic, body(): grad_scores = (probs * (grad_probs - row_dot)).astype(jnp.bfloat16)  26.4 us
    dot_general x1, matrix products, body(): jnp.dot(first_low, inner_weight, preferred_element_type=jnp.float32)  23.8 us
  transfers between devices with their start and end apart: 3, of which 3 were waited for; matrix products, arithmetic and copies ran while one was open for 2% of the time, Pallas kernels for 0%

profile of v1, /device:TPU:0, one launch (start us, length us, event | category | flops | bytes accessed | tf_op | source)
XLA Modules:
  0.0 1052.4 jit_solution(1884869944631554155)
XLA Ops:
  7.3 0.8 fusion.61
  9.5 2.3 copy.70
  11.8 2.2 add_convert_fusion.2
  16.4 3.2 fusion.79
  19.7 3.5 fusion.1
  23.2 2.2 copy-done.2
  25.4 3.8 fusion.35
  29.2 3.2 fusion.80
  32.4 3.5 fusion
  36.0 2.2 copy-done.3
  38.2 4.0 fusion.34
  42.4 1.0 copy-done.23
  44.5 23.8 %multiply_convert_fusion.2 = (bf16[1024,2048]{1,0:T(8,128)(2,1)S(1)}, f32[1024,2048]{1,0:T(8,128)}, f32[1024,2048]{1,0:T(8,128)}) fusion(f32[2048]{0:T(1024)S(1)} %copy-done.62, bf16[512,2048]{1,0:T(8,128)(2,1)S(1)} %copy-done, f32[1024,512]{0,1:T(8,128)S(1)} %get-tuple-element.143, f32[512]{0:T(512)S(1)} %copy-done.66, f32[512]{0:T(512)S(1)} %copy-done.56, ...), kind=kOutput, calls=%fused_computation.27 | convolution fusion | flops 2288517120 | bytes 25186304 | tf_op jit(solution)/shard_map/dot_general | solution.py:121
  68.4 2.7 fusion.82
  71.5 1.0 copy-done.5
  72.9 1.3 copy.72
  74.2 1.9 gather_fusion.1
  76.1 2.0 gather_fusion
  78.1 71.2 %all-gather.1 = bf16[32,5,512]{2,1,0:T(8,128)(2,1)S(1)} all-gather(bf16[1,5,512]{2,1,0:T(8,128)(2,1)S(1)} %bitcast.146), channel_id=2, replica_groups=mesh['side'=4,'batch'=8] {'side','batch'}, dimensions={0}, use_global_device_ids=true | all-gather | bytes 168960 | tf_op jit(solution)/shard_map/all_gather | solution.py:132
  151.0 1.0 fusion.56
  153.0 2.2 scatter_custom_fusion
  155.2 2.9 copy.74
  158.1 115.9 %all-reduce.10.cloned.1.call-done = f32[160,512]{1,0:T(8,128)} async-done(((f32[160,512]{1,0:T(8,128)}), f32[160,512]{1,0:T(8,128)}) %all-reduce.10.cloned.1.call-update) | async-done | bytes 327696
  274.0 2.3 scatter_custom_fusion.1
  276.2 3.0 copy.75
  279.3 3.9 multiply_reduce_fusion.2
  283.2 1.3 fusion.71
  285.3 4.5 fusion.52
  289.9 9.7 fusion.83
  299.6 3.7 multiply_reduce_fusion.3
  303.3 4.5 fusion.18
  307.8 1.4 fusion.72
  309.2 1.7 fusion.49
  311.7 0.9 fusion.76
  313.1 9.3 multiply_reduce_fusion.1
  322.4 15.9 %multiply_convert_fusion.1 = bf16[8,512,1024]{2,1,0:T(8,128)(2,1)} fusion(f32[8,512,1024]{2,1,0:T(8,128)} %get-tuple-element.150, f32[8,512,1024]{2,1,0:T(8,128)} %copy-done.3, f32[8,512]{1,0:T(8,128)S(1)} %get-tuple-element.149, f32[8,512]{1,0:T(8,128)S(1)} %log_add_fusion.1), kind=kLoop, calls=%fused_computation.7 | loop fusion | flops 16777216 | bytes 41975808 | tf_op jit(solution)/shard_map/convert_element_type | solution.py:213
  338.3 8.2 fusion.74
  346.5 6.3 fusion.84
  352.9 4.0 fusion.5
  356.9 9.8 multiply_reduce_fusion
  366.8 8.8 bitcast_reduce_fusion
  375.6 1.7 convolution_bitcast_fusion
  377.3 10.5 multiply_convert_fusion
  387.8 6.3 fusion.75
  394.2 3.4 multiply_convert_fusion.3
  397.5 1.7 convolution_bitcast_fusion.1
  399.2 1.7 convolution_bitcast_fusion.2
  401.0 403.9 %all-reduce.12.cloned.1.call-done = (f32[512,512]{0,1:T(8,128)}, f32[512,512]{0,1:T(8,128)}, f32[512,512]{0,1:T(8,128)}, f32[512,512]{1,0:T(8,128)}, f32[512,2048]{1,0:T(8,128)}, /*index=5*/f32[2048,512]{1,0:T(8,128)}) async-done(((f32[512,512]{0,1:T(8,128)}, f32[512,512]{0,1:T(8,128)}, f32[512,512]{0,1:T(8,128)}, f32[512,512]{1,0:T(8,128)}, f32[512,2048]{1,0:T(8,128)}, /*index=5*/f32[2048,512]{1,0:T(8,128)}), ...) | async-done | bytes 12582928 | tf_op jit(solution)/shard_map/psum | solution.py:256
  804.9 1.6 copy-done.7
  806.6 1.3 fusion.134
  807.9 2.3 copy.80
  810.4 34.5 %all-reduce.2 = (f32[]{:T(128)}, f32[]{:T(128)}, f32[512]{0:T(512)S(1)}, f32[512]{0:T(512)S(1)}, f32[512]{0:T(512)S(1)}, /*index=5*/f32[512]{0:T(512)S(1)}, f32[...) all-reduce(f32[]{:T(128)} %get-tuple-element.81, ...), channel_id=1, replica_groups=mesh['side'=4,'batch'=8] {'batch'}, use_global_device_ids=true, to_apply=%region_11.12 | all-reduce | flops 6146 | bytes 49168 | tf_op jit(solution)/shard_map/psum | solution.py:256
  844.9 13.0 %all-reduce.4 = (f32[]{:T(128)}, f32[]{:T(128)}, f32[512]{0:T(512)}, f32[512]{0:T(512)}, f32[512]{0:T(512)}, /*index=5*/f32[512]{0:T(512)}, f32[512]{0:T(512)}, ...) all-reduce(f32[]{:T(128)} %get-tuple-element.84, ...), channel_id=1, replica_groups=mesh['side'=4,'batch'=8] {'side'}, use_global_device_ids=true, to_apply=%region_12.13 | all-reduce | flops 6146 | bytes 49168 | tf_op jit(solution)/shard_map/psum | solution.py:278
  857.8 1.4 pad_maximum_fusion.1
  859.3 1.9 fusion.86
  861.2 1.8 fusion.85
  863.8 1.3 copy.81
  866.5 163.4 %all-reduce.14.cloned.1.call-done = (f32[512,512]{0,1:T(8,128)}, f32[512,512]{0,1:T(8,128)}, f32[512,512]{0,1:T(8,128)}, f32[512,512]{1,0:T(8,128)}, f32[512,2048]{1,0:T(8,128)}, /*index=5*/f32[2048,512]{1,0:T(8,128)}) async-done(((f32[512,512]{0,1:T(8,128)}, f32[512,512]{0,1:T(8,128)}, f32[512,512]{0,1:T(8,128)}, f32[512,512]{1,0:T(8,128)}, f32[512,2048]{1,0:T(8,128)}, /*index=5*/f32[2048,512]{1,0:T(8,128)}), ...) | async-done | bytes 12582928 | tf_op jit(solution)/shard_map/psum | solution.py:278
  1029.9 2.7 copy.82
  1032.6 2.5 copy.83
  1035.1 1.3 copy.84
  1036.4 1.0 copy.103
  1037.4 4.8 copy.104
  1042.2 2.0 copy.105
  (191 shorter events, 11.7 us)
Async XLA Ops:
  7.2 37.3 %copy-start = (bf16[512,2048]{1,0:T(8,128)(2,1)S(1)}, bf16[512,2048]{1,0:T(8,128)(2,1)}, u32[]{:S(2)}) copy-start(bf16[512,2048]{1,0:T(8,128)(2,1)} %param.38) | copy-start | bytes 6291460
  7.2 6.9 copy-start.27
  7.2 266.8 %all-reduce.10.cloned.1.call-start = ((), (), s32[]{:S(2)}) async-start(), calls=%async_computation | async-start | bytes 655360
  14.2 5.5 copy-start.14
  14.2 15.0 %copy-start.16 = (bf16[512,512]{0,1:T(8,128)(2,1)}, bf16[512,512]{0,1:T(8,128)(2,1)S(1)}, u32[]{:S(2)}) copy-start(bf16[512,512]{0,1:T(8,128)(2,1)S(1)} %get-tuple-element.132) | copy-start | bytes 1572868
  15.0 14.3 %copy-start.10 = (bf16[1024,512]{0,1:T(8,128)(2,1)}, bf16[1024,512]{0,1:T(8,128)(2,1)S(1)}, u32[]{:S(2)}) copy-start(bf16[1024,512]{0,1:T(8,128)(2,1)S(1)} %convolution_convert_fusion.1) | copy-start | bytes 3145732
  15.7 20.2 %copy-start.19 = (bf16[1024,512]{0,1:T(8,128)(2,1)}, bf16[1024,512]{0,1:T(8,128)(2,1)S(1)}, u32[]{:S(2)}) copy-start(bf16[1024,512]{0,1:T(8,128)(2,1)S(1)} %add_convert_fusion.3) | copy-start | bytes 3145732
  19.7 5.7 copy-start.2
  32.4 5.7 copy-start.3
  38.2 5.2 copy-start.32
  38.2 5.2 copy-start.33
  38.2 5.2 copy-start.64
  44.2 24.2 %copy-start.12 = (f32[1024,512]{0,1:T(8,128)}, f32[1024,512]{0,1:T(8,128)S(1)}, u32[]{:S(2)}) copy-start(f32[1024,512]{0,1:T(8,128)S(1)} %get-tuple-element.143) | copy-start | bytes 6291460
  44.5 23.9 %copy-start.60 = (bf16[2048,512]{1,0:T(8,128)(2,1)S(1)}, bf16[2048,512]{1,0:T(8,128)(2,1)}, u32[]{:S(2)}) copy-start(bf16[2048,512]{1,0:T(8,128)(2,1)} %param.40) | copy-start | bytes 6291460
  44.5 23.9 %copy-start.65 = (f32[512]{0:T(512)S(1)}, f32[512]{0:T(512)}, u32[]{:S(2)}) copy-start(f32[512]{0:T(512)} %param.41) | copy-start | bytes 6148
  68.4 4.1 copy-start.42
  68.4 4.1 copy-start.48
  71.1 78.3 %copy-start.55 = (s32[32]{0:T(128)S(1)}, s32[32]{0:T(128)}, u32[]{:S(2)}) copy-start(s32[32]{0:T(128)} %param.26) | copy-start | bytes 388
  71.2 78.2 %copy-start.59 = (s32[120]{0:T(128)S(1)}, s32[120]{0:T(128)}, u32[]{:S(2)}) copy-start(s32[120]{0:T(128)} %param.27) | copy-start | bytes 1444
  71.2 79.1 %copy-start.47 = (f32[32,120]{1,0:T(8,128)S(1)}, f32[32,120]{1,0:T(8,128)}, u32[]{:S(2)}) copy-start(f32[32,120]{1,0:T(8,128)} %param.28) | copy-start | bytes 46084
  152.1 652.8 %all-reduce.12.cloned.1.call-start = ((), (), s32[]{:S(2)}) async-start(), calls=%async_computation.1 | async-start | bytes 25165824 | tf_op jit(solution)/shard_map/psum | solution.py:256
  279.3 3.9 copy-start.6
  285.3 4.5 copy-start.61
  289.9 9.7 copy-start.13
  303.2 9.3 slice-start.4
  303.3 9.3 slice-start.5
  307.8 3.2 copy-start.34
  307.8 4.8 slice-start.6
  309.2 3.3 copy-start.8
  309.2 3.9 slice-start.7
  322.3 16.0 %copy-start.11 = (bf16[1024,512]{0,1:T(8,128)(2,1)S(1)}, bf16[1024,512]{0,1:T(8,128)(2,1)}, u32[]{:S(2)}) copy-start(bf16[1024,512]{0,1:T(8,128)(2,1)} %copy-done.10) | copy-start | bytes 3145732
  322.3 30.5 %slice-start = ((s8[16777216]{0:T(1024)(128)(4,1)}), s8[4194304]{0:T(1024)(128)(4,1)S(1)}, s32[]{:S(2)}) async-start(s8[16777216]{0:T(1024)(128)(4,1)} %bitcast.117), calls=%async_computation.3 | async-start | bytes 8388608
  322.3 30.5 %slice-start.1 = ((s8[16777216]{0:T(1024)(128)(4,1)}), s8[4194304]{0:T(1024)(128)(4,1)S(1)}, s32[]{:S(2)}) async-start(s8[16777216]{0:T(1024)(128)(4,1)} %bitcast.117), calls=%async_computation.4 | async-start | bytes 8388608
  322.4 30.5 %slice-start.2 = ((s8[16777216]{0:T(1024)(128)(4,1)}), s8[4194304]{0:T(1024)(128)(4,1)S(1)}, s32[]{:S(2)}) async-start(s8[16777216]{0:T(1024)(128)(4,1)} %bitcast.117), calls=%async_computation.5 | async-start | bytes 8388608
  338.3 8.2 copy-start.17
  338.3 14.5 %slice-start.3 = ((s8[16777216]{0:T(1024)(128)(4,1)}), s8[4194304]{0:T(1024)(128)(4,1)S(1)}, s32[]{:S(2)}) async-start(s8[16777216]{0:T(1024)(128)(4,1)} %bitcast.117), calls=%async_computation.6 | async-start | bytes 8388608
  346.5 6.4 copy-start.18
  346.5 6.4 copy-start.38
  352.9 4.1 copy-start.39
  366.8 8.8 copy-start.28
  366.8 10.5 %copy-start.40 = (f32[8,512]{1,0:T(8,128)S(1)}, f32[8,512]{1,0:T(8,128)}, u32[]{:S(2)}) copy-start(f32[8,512]{1,0:T(8,128)} %log_add_fusion) | copy-start | bytes 49156
  366.8 10.5 %copy-start.41 = (f32[8,512]{1,0:T(8,128)S(1)}, f32[8,512]{1,0:T(8,128)}, u32[]{:S(2)}) copy-start(f32[8,512]{1,0:T(8,128)} %get-tuple-element.151) | copy-start | bytes 49156
  387.8 6.3 copy-start.4
  387.8 6.3 copy-start.15
  394.1 5.1 copy-start.26
  394.1 3.4 copy-start.29
  394.1 5.1 copy-start.25
  400.9 629.0 %all-reduce.14.cloned.1.call-start = ((), (), s32[]{:S(2)}) async-start(), calls=%async_computation.2 | async-start | bytes 25165824 | tf_op jit(solution)/shard_map/psum | solution.py:278
  806.5 3.7 copy-start.46
  806.5 3.8 copy-start.44
  806.5 3.8 copy-start.50
  806.5 3.8 copy-start.51
  806.5 3.8 copy-start.52
  806.5 3.8 copy-start.53
  806.5 3.8 copy-start.54
  806.5 3.8 copy-start.57
  806.6 3.8 copy-start.58
  859.2 3.7 copy-start.9
  859.2 3.7 copy-start.21
  859.3 3.7 copy-start.37
  1029.9 5.2 copy-start.31
  1029.9 6.5 copy-start.30
  1037.4 4.9 copy-start.22
  1037.4 6.9 copy-start.1
  (16 other events, 32.4 us)
Sparse Core Ops, SparseCore 0:
  152.2 121.7 all-reduce.9
  401.1 403.7 all-reduce.11
  808.0 221.8 all-reduce.13
